TPU v7x, 1024 devices: a whole 4x4x32 slice. The times are simulated.
1024 devices in a mesh: dp: 16 (over x, y), proto: 64 (over z, core).
Axes of the slice: x: 4, y: 4, z: 32, core: 2. Of those that a mesh axis runs over, the one named last changes fastest.
Arguments:
- teacher_feat: bfloat16 [8192, 256], P('dp'), may hold values from -8 to 8
- small_feat: bfloat16 [8192, 256], P('dp'), may hold values from -6 to 6
- large_feat: bfloat16 [8192, 256], P('dp'), may hold values from -6 to 6
- teacher_proto: bfloat16 [256, 65536], P(None, 'proto'), may hold values from -4 to 4
- small_proto: bfloat16 [256, 65536], P(None, 'proto'), may hold values from -6 to 6
- large_proto: bfloat16 [256, 65536], P(None, 'proto'), may hold values from -6 to 6
Outputs:
- small_proto_grad: float32 [256, 65536], P('dp', 'proto')
- large_proto_grad: float32 [256, 65536], P('dp', 'proto')
- small_feat_grad: float32 [8192, 256], P('dp')
- large_feat_grad: float32 [8192, 256], P('dp')
All inputs are finite; a program needn't handle non-finite values.
Results may differ from a plain program's by a relative error of at most 0.012.
The roundings to bfloat16 on the way count: a program that leaves them out, or rounds other values in their place, can miss the bound.
Values sent between devices are 32-bit elements; how exact they have to be, the bound alone decides.
A program may use at most 32 MiB of HBM per device.

v0:
```python
import jax
import jax.numpy as jnp
from jax import lax
from jax.sharding import PartitionSpec as P

ITERS = 3


teacher_temp = 0.07
student_temp = 0.1
loss_scale = 4096.0


def sent_to_all(array, axis):
    copies = jnp.broadcast_to(array, (lax.axis_size(axis), *array.shape))
    return lax.all_to_all(copies, axis, split_axis=0, concat_axis=0, tiled=True)


def taken_together(array, axis):
    everything = sent_to_all(array, axis)
    return jnp.sum(everything, axis=0)


def in_one(arrays, axis):
    ends = [0]
    for a in arrays:
        ends.append(ends[-1] + a.size)
    subtotal = taken_together(jnp.concatenate([a.ravel() for a in arrays]), axis)
    return tuple((subtotal[b:e].reshape(a.shape) for a, b, e in zip(arrays, ends, ends[1:])))


def in_blocks(array, dim, peers):
    lengths = array.shape
    parts = array.reshape(*lengths[:dim], peers, lengths[dim] // peers, *lengths[dim + 1 :])
    return jnp.moveaxis(parts, dim, 0)


def sum_at_owner(array, axis, dim):
    peers = lax.axis_size(axis)
    parts = lax.all_to_all(in_blocks(array, dim, peers), axis, 0, 0, tiled=True)
    return jnp.sum(parts, axis=0)


def in_one_piece(arrays, axis, dim, along):
    widths = [a.shape[along] for a in arrays]
    both = jnp.concatenate(arrays, axis=along)
    whole = sum_at_owner(both, axis, dim)
    return tuple(jnp.split(whole, [sum(widths[:k]) for k in range(1, len(widths))], axis=along))


def unit_rows(features):
    values = features.astype(jnp.float32)
    inv_norm = lax.rsqrt(jnp.sum(values * values, axis=1, keepdims=True) + 1e-12)
    return (values * inv_norm, inv_norm)


def unit_columns(prototypes):
    values = prototypes.astype(jnp.float32)
    inv_norm = lax.rsqrt(jnp.sum(values * values, axis=0, keepdims=True) + 1e-12)
    return (values * inv_norm).astype(jnp.bfloat16)


def column_totals(partial_value):
    return taken_together(partial_value, "dp")


def row_totals(partial_value):
    return taken_together(partial_value, "proto")


def unit_back(back, unit_f, inv_norm):
    return (back - unit_f * jnp.sum(unit_f * back, axis=1, keepdims=True)) * inv_norm


def on_device(teacher_feat, small_feat, large_feat, teacher_proto, small_proto, large_proto):
    teacher_unit = unit_rows(teacher_feat)[0].astype(jnp.bfloat16)
    energy = jnp.exp(
        jnp.dot(teacher_unit, unit_columns(teacher_proto), preferred_element_type=jnp.float32)
        / teacher_temp
    )
    small_f, small_inv = unit_rows(small_feat)
    large_f, large_inv = unit_rows(large_feat)
    small_unit = small_f.astype(jnp.bfloat16)
    large_unit = large_f.astype(jnp.bfloat16)
    small_cols = unit_columns(small_proto)
    large_cols = unit_columns(large_proto)
    small_expo = jnp.exp(
        jnp.dot(small_unit, small_cols, preferred_element_type=jnp.float32) / student_temp
    )
    large_expo = jnp.exp(
        jnp.dot(large_unit, large_cols, preferred_element_type=jnp.float32) / student_temp
    )
    small_part = jnp.sum(small_expo, axis=1)
    large_part = jnp.sum(large_expo, axis=1)
    crop_scale = jnp.ones((energy.shape[0],), jnp.float32)
    proto_scale = jnp.ones((energy.shape[1],), jnp.float32)
    small_total = small_part
    large_total = large_part
    for sweep_index in range(ITERS):
        proto_scale = 1.0 / column_totals(
            jnp.dot(crop_scale, energy, precision=lax.Precision.HIGHEST)
        )
        local_rows = jnp.dot(energy, proto_scale, precision=lax.Precision.HIGHEST)
        if sweep_index == 0:
            row_sum, small_total, large_total = in_one(
                (local_rows, small_part, large_part), "proto"
            )
        else:
            row_sum = row_totals(local_rows)
        crop_scale = 1.0 / row_sum
    target = crop_scale[:, None] * energy * proto_scale[None, :]
    small_grad = (loss_scale / student_temp * (small_expo / small_total[:, None] - target)).astype(
        jnp.bfloat16
    )
    large_grad = (loss_scale / student_temp * (large_expo / large_total[:, None] - target)).astype(
        jnp.bfloat16
    )
    outputs = []
    for unit_b, grad_b in ((small_unit, small_grad), (large_unit, large_grad)):
        outputs.append(
            lax.dot_general(
                unit_b, grad_b, (((0,), (0,)), ((), ())), preferred_element_type=jnp.float32
            )
        )
    combined = sum_at_owner(jnp.concatenate(outputs, axis=1), "dp", 0)
    grad_width = small_grad.shape[1]
    small_proto_grad = combined[:, :grad_width]
    large_proto_grad = combined[:, grad_width:]
    contract = (((1,), (1,)), ((), ()))
    small_back = lax.dot_general(
        small_grad, small_cols, contract, preferred_element_type=jnp.float32
    )
    large_back = lax.dot_general(
        large_grad, large_cols, contract, preferred_element_type=jnp.float32
    )
    small_sum, large_sum = in_one_piece((small_back, large_back), "proto", 0, 1)
    share_rows = small_sum.shape[0]
    first_share = lax.axis_index("proto") * share_rows
    small_out = unit_back(
        small_sum,
        lax.dynamic_slice_in_dim(small_f, first_share, share_rows, 0),
        lax.dynamic_slice_in_dim(small_inv, first_share, share_rows, 0),
    )
    large_out = unit_back(
        large_sum,
        lax.dynamic_slice_in_dim(large_f, first_share, share_rows, 0),
        lax.dynamic_slice_in_dim(large_inv, first_share, share_rows, 0),
    )
    small_feat_grad, large_feat_grad = (
        lax.all_gather(small_out, "proto", axis=0, tiled=True),
        lax.all_gather(large_out, "proto", axis=0, tiled=True),
    )
    return (small_proto_grad, large_proto_grad, small_feat_grad, large_feat_grad)


def solution(mesh):
    placed = (
        P("dp", None),
        P("dp", None),
        P("dp", None),
        P(None, "proto"),
        P(None, "proto"),
        P(None, "proto"),
    )
    return jax.shard_map(
        on_device,
        mesh=mesh,
        in_specs=placed,
        out_specs=(P("dp", "proto"), P("dp", "proto"), P("dp", None), P("dp", None)),
        check_vma=False,
    )
```

profile of v0, /device:TPU:1, one launch (start us, length us, event | category | flops | bytes accessed | tf_op | source)
XLA Modules:
  0.0 474.4 jit_solution(11635487210500681380)
XLA Ops:
  0.6 1.2 fusion.4
  1.8 1.1 fusion.9
  2.9 1.7 multiply_exponential_fusion.1
  4.7 1.1 fusion.30
  5.7 0.7 broadcast_in_dim.12
  6.4 7.6 %all-to-all-start = ((f32[16,1,1024]{2,1,0:T(1,128)}), f32[16,1,1024]{2,1,0:T(1,128)S(1)}, u32[]{:S(2)}, u32[]{:S(2)}) async-start(f32[16,1,1024]{2,1,0:T(1,128)} %broadcast_in_dim.12), calls=%async_computation | async-start | bytes 131072 | tf_op jit(solution)/shard_map/all_to_all | solution.py:16
  14.0 0.1 fusion.11
  14.2 0.1 fusion.6
  14.3 0.1 fusion.8
  14.5 1.2 fusion.2
  15.7 1.8 fusion.1
  17.5 1.8 fusion
  19.3 1.2 all-to-all-done
  20.6 1.9 fusion.35
  22.5 0.2 broadcast_in_dim.13
  22.7 84.0 %all_to_all.46 = f32[64,1,1536]{2,1,0:T(1,128)S(1)} all-to-all(f32[64,1,1536]{2,1,0:T(1,128)S(1)} %broadcast_in_dim.13), channel_id=1, replica_groups=mesh['dp'=16,'proto'=64] {'proto'}, dimensions={0} | all-to-all | bytes 786432 | tf_op jit(solution)/shard_map/all_to_all | solution.py:16
  106.7 0.2 reduce_sum.171
  107.0 1.1 fusion.36
  108.1 10.9 %all_to_all.47 = f32[16,1,1024]{2,1,0:T(1,128)S(1)} all-to-all(f32[16,1,1024]{2,1,0:T(1,128)S(1)} %broadcast_in_dim.14), channel_id=1, replica_groups=mesh['dp'=16,'proto'=64] {'dp'}, dimensions={0} | all-to-all | bytes 131072 | tf_op jit(solution)/shard_map/all_to_all | solution.py:16
  119.1 1.9 fusion.37
  121.0 37.4 %all_to_all.48 = f32[64,1,512]{2,1,0:T(1,128)S(1)} all-to-all(f32[64,1,512]{2,1,0:T(1,128)S(1)} %broadcast_in_dim.15), channel_id=1, replica_groups=mesh['dp'=16,'proto'=64] {'proto'}, dimensions={0} | all-to-all | bytes 262144 | tf_op jit(solution)/shard_map/all_to_all | solution.py:16
  158.4 0.1 reduce_sum.173
  158.5 1.1 fusion.38
  159.7 9.5 %all_to_all.49 = f32[16,1,1024]{2,1,0:T(1,128)S(1)} all-to-all(f32[16,1,1024]{2,1,0:T(1,128)S(1)} %broadcast_in_dim.16), channel_id=1, replica_groups=mesh['dp'=16,'proto'=64] {'dp'}, dimensions={0} | all-to-all | bytes 131072 | tf_op jit(solution)/shard_map/all_to_all | solution.py:16
  169.2 1.9 fusion.39
  171.2 37.3 %all_to_all.50 = f32[64,1,512]{2,1,0:T(1,128)S(1)} all-to-all(f32[64,1,512]{2,1,0:T(1,128)S(1)} %broadcast_in_dim.17), channel_id=1, replica_groups=mesh['dp'=16,'proto'=64] {'proto'}, dimensions={0} | all-to-all | bytes 262144 | tf_op jit(solution)/shard_map/all_to_all | solution.py:16
  208.4 0.1 reduce_sum.175
  208.5 2.8 multiply_convert_fusion.1
  211.4 0.6 fusion.27
  211.9 0.6 copy-done.3
  212.5 0.6 fusion.24
  213.1 1.6 pad_maximum_fusion
  214.6 3.7 all-to-all-start.6
  218.4 1.9 fusion.14
  220.3 0.5 fusion.18
  220.9 1.3 copy.18
  222.2 22.0 %all-to-all-done.6 = f32[16,16,2048]{2,1,0:T(8,128)S(1)} async-done(((f32[16,16,2048]{2,1,0:T(8,128)}), f32[16,16,2048]{2,1,0:T(8,128)S(1)}, u32[]{:S(2)}, u32[]{:S(2)}) %all-to-all-start.6) | async-done | bytes 2097184 | tf_op jit(solution)/shard_map/all_to_all | solution.py:40
  244.2 9.2 %all-to-all-start.7 = ((f32[64,8,512]{2,1,0:T(8,128)}), f32[64,8,512]{2,1,0:T(8,128)S(1)}, u32[]{:S(2)}, u32[]{:S(2)}) async-start(f32[64,8,512]{2,1,0:T(8,128)} %bitcast.12), calls=%async_computation.7 | async-start | bytes 2097152 | tf_op jit(solution)/shard_map/all_to_all | solution.py:40
  253.5 2.1 convert_multiply_fusion.6
  255.6 0.1 reduce_sum.176
  255.7 0.7 fusion.33
  256.4 104.9 %all-to-all-done.7 = f32[64,8,512]{2,1,0:T(8,128)S(1)} async-done(((f32[64,8,512]{2,1,0:T(8,128)}), f32[64,8,512]{2,1,0:T(8,128)S(1)}, u32[]{:S(2)}, u32[]{:S(2)}) %all-to-all-start.7) | async-done | bytes 1048608 | tf_op jit(solution)/shard_map/all_to_all | solution.py:40
  361.4 0.9 multiply_reduce_fusion
  362.2 0.8 subtract_multiply_fusion
  363.0 55.4 %all_gather.6 = f32[512,256]{1,0:T(8,128)S(1)} all-gather(f32[8,256]{1,0:T(8,128)S(1)} %get-tuple-element.11), channel_id=1, replica_groups=mesh['dp'=16,'proto'=64] {'proto'}, dimensions={0}, use_global_device_ids=true | all-gather | bytes 532480 | tf_op jit(solution)/shard_map/all_gather | solution.py:150
  418.4 54.4 %all_gather.7 = f32[512,256]{1,0:T(8,128)S(1)} all-gather(f32[8,256]{1,0:T(8,128)S(1)} %get-tuple-element.10), channel_id=1, replica_groups=mesh['dp'=16,'proto'=64] {'proto'}, dimensions={0}, use_global_device_ids=true | all-gather | bytes 532480 | tf_op jit(solution)/shard_map/all_gather | solution.py:151
  472.8 0.8 copy.30
  473.6 0.8 copy.31
  (37 shorter events, 0.8 us)
Async XLA Ops:
  2.9 11.1 %copy-start.2 = (bf16[512,256]{1,0:T(8,128)(2,1)S(1)}, bf16[512,256]{1,0:T(8,128)(2,1)}, u32[]{:S(2)}) copy-start(bf16[512,256]{1,0:T(8,128)(2,1)} %param.8) | copy-start | bytes 786436
  2.9 11.2 %copy-start.4 = (bf16[256,1024]{1,0:T(8,128)(2,1)S(1)}, bf16[256,1024]{1,0:T(8,128)(2,1)}, u32[]{:S(2)}) copy-start(bf16[256,1024]{1,0:T(8,128)(2,1)} %param.11) | copy-start | bytes 1572868
  4.6 9.7 %copy-start.1 = (bf16[512,256]{1,0:T(8,128)(2,1)S(1)}, bf16[512,256]{1,0:T(8,128)(2,1)}, u32[]{:S(2)}) copy-start(bf16[512,256]{1,0:T(8,128)(2,1)} %param.7) | copy-start | bytes 786436
  6.4 14.1 %all-to-all-start = ((f32[16,1,1024]{2,1,0:T(1,128)}), f32[16,1,1024]{2,1,0:T(1,128)S(1)}, u32[]{:S(2)}, u32[]{:S(2)}) async-start(f32[16,1,1024]{2,1,0:T(1,128)} %broadcast_in_dim.12), calls=%async_computation | async-start | bytes 131072 | tf_op jit(solution)/shard_map/all_to_all | solution.py:16
  14.2 3.3 copy-start.5
  211.3 1.7 copy-start
  211.4 1.1 copy-start.3
  214.6 29.5 %all-to-all-start.6 = ((f32[16,16,2048]{2,1,0:T(8,128)}), f32[16,16,2048]{2,1,0:T(8,128)S(1)}, u32[]{:S(2)}, u32[]{:S(2)}) async-start(f32[16,16,2048]{2,1,0:T(8,128)} %bitcast.28), calls=%async_computation.6 | async-start | bytes 4194304 | tf_op jit(solution)/shard_map/all_to_all | solution.py:40
  218.4 1.9 copy-start.6
  244.2 117.1 %all-to-all-start.7 = ((f32[64,8,512]{2,1,0:T(8,128)}), f32[64,8,512]{2,1,0:T(8,128)S(1)}, u32[]{:S(2)}, u32[]{:S(2)}) async-start(f32[64,8,512]{2,1,0:T(8,128)} %bitcast.12), calls=%async_computation.7 | async-start | bytes 2097152 | tf_op jit(solution)/shard_map/all_to_all | solution.py:40
where the time goes:
time: 475 us; the launch traced here: 474 us
  blocking collectives  289 us (61%)
  waiting for transfers between devices  128 us (27%)
  starting transfers between devices  20.5 us (4%)
  matrix products  17.7 us (4%)
  other arithmetic  13 us (3%)
  local copies, waits for them, and re-layouts  5.44 us (1%)
    all_to_all x5, blocking collectives, sent_to_all(): return lax.all_to_all(copies, axis, split_axis=0, concat_axis=0, tiled=True)  179 us
    all_to_all x2, waiting for transfers between devices, sum_at_owner(): parts = lax.all_to_all(in_blocks(array, dim, peers), axis, 0, 0, tiled=True)  127 us
    all_gather x1, blocking collectives, on_device(): lax.all_gather(small_out, 'proto', axis=0, tiled=True)  55.4 us
    all_gather x1, blocking collectives, on_device(): lax.all_gather(large_out, 'proto', axis=0, tiled=True)  54.4 us
    all_to_all x2, starting transfers between devices, sum_at_owner(): parts = lax.all_to_all(in_blocks(array, dim, peers), axis, 0, 0, tiled=True)  12.9 us
  transfers between devices with their start and end apart: 3, of which 3 were waited for; matrix products, arithmetic and copies ran while one was open for 3% of the time, Pallas kernels for 0%

commit v1 on v0

v1 whole, which is shorter than its diff:
```python
import jax
import jax.numpy as jnp
from jax import lax
from jax.experimental import pallas as pl
from jax.experimental.pallas import tpu as pltpu
from jax.sharding import PartitionSpec as P

MESH = pl.DeviceIdType.MESH
F32 = jnp.float32
BF16 = jnp.bfloat16

ITERS = 3
LOG2E = 1.4426950408889634
TEACHER_EXPONENT = LOG2E / 0.07
STUDENT_EXPONENT = LOG2E / 0.1
GRAD_SCALE = 4096.0 / 0.1

ROWS = 512
BOT = 256
COLS = 1024
TILE = 128
WIDE = 256
DP = 16
NZ = 32
CONTRACT_LAST = (((1,), (1,)), ((), ()))


def kernel(
    tf, sf, lf, tp, sp, lp,
    pgs_out, pgl_out, fgs_out, fgl_out,
    energy, expo_s, expo_l, cols_t, cols_s, cols_l,
    unit_t, unit_s, unit_l, unit_st, unit_lt, acc, grad_s, grad_l, inv_total_ref,
    dp_own, dp_got, win_own, win_got, far_own, far_got,
    tot_own, totw_got, totf_own, totf_got,
    back, core_got, rsw_own, rsw_got, rsf_own, rsf_got,
    fin, agf_got, half, other, pg, pg_got,
    dp_ss, dp_rs, win_ss, win_rs, far_ss, far_rs, core_ss, core_rs,
    rsw_ss, rsw_rs, rsf_ss, rsf_rs, agf_ss, agf_rs, agw_ss, agw_rs, fwd_ss, fwd_rs, pg_ss, pg_rs,
):
    dp = lax.axis_index("dp")
    pr = lax.axis_index("proto")
    x, y = lax.div(dp, 4), lax.rem(dp, 4)
    z, core = lax.div(pr, 2), lax.rem(pr, 2)

    def dp_peer(k):
        px = lax.rem(x + lax.div(k, 4), 4)
        py = lax.rem(y + lax.rem(k, 4), 4)
        return px * 4 + py

    def z_at(offset):
        return lax.rem(z + offset + NZ, NZ)

    def near(w):
        return w - 3 + lax.div(w + 5, 8)

    def far(f):
        return 8 * f - 12

    def remote(src, dst, ss, rs, to_dp, to_z, to_core):
        return pltpu.make_async_remote_copy(
            src_ref=src, dst_ref=dst, send_sem=ss, recv_sem=rs,
            device_id=(to_dp, to_z * 2 + to_core), device_id_type=MESH,
        )

    def each(lo, hi, make):
        def go(k, carry):
            make(k).start()
            return carry
        lax.fori_loop(lo, hi, go, 0)

    def settle(lo, hi, make):
        def go(k, carry):
            make(k).wait()
            return carry
        lax.fori_loop(lo, hi, go, 0)

    barrier = pltpu.get_barrier_semaphore()

    def greet(to_dp, to_z, to_core):
        pl.semaphore_signal(
            barrier, inc=1, device_id=(to_dp, to_z * 2 + to_core), device_id_type=MESH
        )

    for offset in (-12, 12, -4, 4):
        greet(dp, z_at(offset), core)
        greet(dp, z_at(offset), 1 - core)
    for offset in (-3, 3, -2, 2, -1, 1):
        greet(dp, z_at(offset), core)
    greet(dp, z, 1 - core)
    for k in range(1, DP):
        greet(dp_peer(k), z, core)

    def units(feat, unit, unit_tr):
        for b in range(0, ROWS, TILE):
            v = feat[b : b + TILE, :].astype(F32)
            u = v * lax.rsqrt(jnp.sum(v * v, axis=1, keepdims=True) + 1e-12)
            unit[b : b + TILE, :] = u.astype(BF16)
            if unit_tr is not None:
                unit_tr[:, b : b + TILE] = u.T.astype(BF16)

    def head(unit, proto, cols, expo, exponent, finish):
        @pl.loop(0, COLS // WIDE)
        def _(j):
            at = pl.ds(pl.multiple_of(j * WIDE, WIDE), WIDE)
            v = proto[:, at].astype(F32)
            c = (v * lax.rsqrt(jnp.sum(v * v, axis=0, keepdims=True) + 1e-12)).astype(BF16)
            cols[:, at] = c
            e = jnp.exp2(jnp.dot(unit[...], c, preferred_element_type=F32) * exponent)
            expo[:, at] = e
            finish(at, e)

    def lane_sums(read, write):
        for b in range(0, ROWS, TILE):
            write(b, jnp.sum(read(b).T, axis=0, keepdims=True))

    def spread(row):
        return jnp.broadcast_to(row, (TILE, TILE)).T

    units(tf, unit_t, None)

    def teacher_finish(at, e):
        dp_own[0, :, at] = jnp.sum(e, axis=0, keepdims=True)

    head(unit_t, tp, cols_t, energy, TEACHER_EXPONENT, teacher_finish)

    def student_finish(at, e):
        acc[...] += e[:, :TILE] + e[:, TILE:]

    for which, (feat, unit, unit_tr, proto, cols, expo) in enumerate(
        ((sf, unit_s, unit_st, sp, cols_s, expo_s), (lf, unit_l, unit_lt, lp, cols_l, expo_l))
    ):
        units(feat, unit, unit_tr)
        acc[...] = jnp.zeros_like(acc)
        head(unit, proto, cols, expo, STUDENT_EXPONENT, student_finish)

        def put(b, row, which=which):
            tot_own[:, which * ROWS + b : which * ROWS + b + TILE] = row

        lane_sums(lambda b: acc[b : b + TILE, :], put)

    pl.semaphore_wait(barrier, 30)

    def tot_window(w):
        return remote(tot_own, totw_got.at[w], win_ss.at[3, w], win_rs.at[3, w], dp, z_at(near(w)), core)

    def tot_far(g):
        f, to_core = lax.div(g, 2), lax.rem(g, 2)
        return remote(
            totf_own, totf_got.at[f * 2 + core], far_ss.at[3, g], far_rs.at[3, f * 2 + core],
            dp, z_at(far(f)), to_core,
        )

    def tot_far_here(g):
        f = lax.div(g, 2)
        return remote(
            totf_own, totf_got.at[g], far_ss.at[3, g], far_rs.at[3, g], dp, z_at(far(f)), lax.rem(g, 2)
        )

    for it in range(ITERS):
        def dp_copy(k, it=it):
            return remote(dp_own.at[it], dp_got.at[it, k], dp_ss.at[it, k], dp_rs.at[it, k], dp_peer(k), z, core)

        def window(w, it=it):
            return remote(win_own.at[it], win_got.at[it, w], win_ss.at[it, w], win_rs.at[it, w], dp, z_at(near(w)), core)

        def far_send(g, it=it):
            f, to_core = lax.div(g, 2), lax.rem(g, 2)
            return remote(
                far_own.at[it], far_got.at[it, f * 2 + core], far_ss.at[it, g], far_rs.at[it, f * 2 + core],
                dp, z_at(far(f)), to_core,
            )

        def far_here(g, it=it):
            f = lax.div(g, 2)
            return remote(
                far_own.at[it], far_got.at[it, g], far_ss.at[it, g], far_rs.at[it, g],
                dp, z_at(far(f)), lax.rem(g, 2),
            )

        each(1, DP, dp_copy)
        settle(1, DP, dp_copy)
        col_total = dp_own[it]
        for k in range(1, DP):
            col_total += dp_got[it, k]
        proto_scale = 1.0 / col_total
        for b in range(0, ROWS, TILE):
            part = energy[b : b + TILE, :TILE] * proto_scale[:, :TILE]
            for c in range(TILE, COLS, TILE):
                part += energy[b : b + TILE, c : c + TILE] * proto_scale[:, c : c + TILE]
            win_own[it, :, b : b + TILE] = jnp.sum(part.T, axis=0, keepdims=True)
        each(0, 7, window)
        if it == 0:
            each(0, 7, tot_window)
        settle(0, 7, window)
        near_total = win_own[it]
        for w in range(7):
            near_total += win_got[it, w]
        far_own[it] = near_total
        each(0, 8, far_send)
        if it == 0:
            settle(0, 7, tot_window)
            tot_near = tot_own[...]
            for w in range(7):
                tot_near += totw_got[w]
            totf_own[...] = tot_near
            each(0, 8, tot_far)
        settle(0, 8, far_here)
        row_total = far_got[it, 0]
        for g in range(1, 8):
            row_total += far_got[it, g]
        crop_scale = 1.0 / row_total
        if it < ITERS - 1:
            sums = [None] * (COLS // TILE)
            for b in range(0, ROWS, TILE):
                along = spread(crop_scale[:, b : b + TILE])
                for c in range(COLS // TILE):
                    part = jnp.sum(
                        along * energy[b : b + TILE, c * TILE : (c + 1) * TILE], axis=0, keepdims=True
                    )
                    sums[c] = part if sums[c] is None else sums[c] + part
            for c in range(COLS // TILE):
                dp_own[it + 1, :, c * TILE : (c + 1) * TILE] = sums[c]

    settle(0, 8, tot_far_here)
    total = totf_got[0]
    for g in range(1, 8):
        total += totf_got[g]
    inv_total_ref[...] = GRAD_SCALE / total
    inv_total = inv_total_ref[...]
    proto_grad_scale = proto_scale * GRAD_SCALE

    for b in range(0, ROWS, TILE):
        along = spread(crop_scale[:, b : b + TILE])
        small_along = spread(inv_total[:, b : b + TILE])
        large_along = spread(inv_total[:, ROWS + b : ROWS + b + TILE])
        for c in range(0, COLS, TILE):
            target = along * energy[b : b + TILE, c : c + TILE] * proto_grad_scale[:, c : c + TILE]
            grad_s[b : b + TILE, c : c + TILE] = (
                expo_s[b : b + TILE, c : c + TILE] * small_along - target
            ).astype(BF16)
            grad_l[b : b + TILE, c : c + TILE] = (
                expo_l[b : b + TILE, c : c + TILE] * large_along - target
            ).astype(BF16)

    half_rows = ROWS // 2
    for i, (grad, cols) in enumerate(((grad_s, cols_s), (grad_l, cols_l))):
        back[:, i * BOT : (i + 1) * BOT] = lax.dot_general(
            grad[...], cols[...], CONTRACT_LAST, preferred_element_type=F32
        )
    mine = pl.multiple_of(core * half_rows, half_rows)
    theirs = pl.multiple_of((1 - core) * half_rows, half_rows)
    to_pair = remote(back.at[pl.ds(theirs, half_rows)], core_got, core_ss.at[0], core_rs.at[0], dp, z, 1 - core)
    to_pair.start()

    for i, (unit_tr, grad) in enumerate(((unit_st, grad_s), (unit_lt, grad_l))):
        for c in range(0, COLS, WIDE):
            pg[:, :, i * COLS + c : i * COLS + c + WIDE] = jnp.dot(
                unit_tr[...], grad[:, c : c + WIDE], preferred_element_type=F32
            ).reshape(DP, BOT // DP, WIDE)

    def pg_copy(k):
        to = dp_peer(k)
        return remote(pg.at[to], pg_got.at[k], pg_ss.at[k], pg_rs.at[k], to, z, core)

    to_pair.wait()

    @pl.loop(0, half_rows // 32)
    def _(i):
        rows = pl.ds(pl.multiple_of(i * 32, 32), 32)
        rsw_own[rows, :] = back[pl.ds(pl.multiple_of(mine + i * 32, 32), 32), :] + core_got[rows, :]

    def class_rows(of_z):
        return pl.ds(pl.multiple_of(lax.rem(of_z + 4, 8) * 32, 32), 32)

    def rs_window(w):
        to_z = z_at(near(w))
        return remote(rsw_own.at[class_rows(to_z)], rsw_got.at[w], rsw_ss.at[w], rsw_rs.at[w], dp, to_z, core)

    each(0, 7, rs_window)
    each(1, DP, pg_copy)
    settle(0, 7, rs_window)
    window_sum = rsw_own[class_rows(z), :]
    for w in range(7):
        window_sum += rsw_got[w]
    rsf_own[...] = window_sum

    def owner_rows(of_z):
        return pl.ds(pl.multiple_of(lax.div(of_z, 8) * 8, 8), 8)

    def rs_far(f):
        to_z = z_at(far(f))
        return remote(rsf_own.at[owner_rows(to_z)], rsf_got.at[f], rsf_ss.at[f], rsf_rs.at[f], dp, to_z, core)

    each(0, 4, rs_far)
    settle(0, 4, rs_far)
    own_back = (rsf_got[0] + rsf_got[1]) + (rsf_got[2] + rsf_got[3])

    first = pl.multiple_of(mine + lax.rem(z, 8) * 32 + lax.div(z, 8) * 8, 8)
    for i, feat in enumerate((sf, lf)):
        v = feat[pl.ds(first, 8), :].astype(F32)
        inv = lax.rsqrt(jnp.sum(v * v, axis=1, keepdims=True) + 1e-12)
        u = v * inv
        b = own_back[:, i * BOT : (i + 1) * BOT]
        fin[:, i * BOT : (i + 1) * BOT] = (b - u * jnp.sum(u * b, axis=1, keepdims=True)) * inv

    def ag_far(f):
        return remote(fin, agf_got.at[owner_rows(z)], agf_ss.at[f], agf_rs.at[f], dp, z_at(far(f)), core)

    def ag_far_here(f):
        return remote(
            fin, agf_got.at[owner_rows(z_at(-far(f)))], agf_ss.at[f], agf_rs.at[f], dp, z_at(far(f)), core
        )

    each(0, 4, ag_far)
    settle(0, 4, ag_far_here)

    def ag_window(w):
        return remote(agf_got, half.at[w], agw_ss.at[w], agw_rs.at[w], dp, z_at(-near(w)), core)

    each(0, 7, ag_window)

    def ag_pair(w):
        return remote(half.at[w], other.at[w], fwd_ss.at[w], fwd_rs.at[w], dp, z, 1 - core)

    own_pair = remote(agf_got, other.at[7], fwd_ss.at[7], fwd_rs.at[7], dp, z, 1 - core)
    own_pair.start()

    def put_rows(from_z, base, value):
        rows = pl.ds(pl.multiple_of(base + lax.rem(from_z + 4, 8) * 32, 32), 32)
        fgs_out[rows, :] = value[:, :BOT]
        fgl_out[rows, :] = value[:, BOT:]

    put_rows(z, mine, agf_got[...])

    settle(1, DP, pg_copy)
    pg_total = pg[dp]
    for k in range(1, DP):
        pg_total += pg_got[k]
    pgs_out[...] = pg_total[:, :COLS]
    pgl_out[...] = pg_total[:, COLS:]

    for w in (2, 3, 1, 4, 0, 5, 6):
        ag_window(w).wait()
        ag_pair(w).start()
        put_rows(z_at(near(w)), mine, half[w])
    own_pair.wait()
    put_rows(z, theirs, other[7])
    for w in (2, 3, 1, 4, 0, 5, 6):
        ag_pair(w).wait()
        put_rows(z_at(near(w)), theirs, other[w])


def on_device(*args):
    dma = pltpu.SemaphoreType.DMA
    vmem = pltpu.VMEM
    pairs = lambda *shape: [dma(shape), dma(shape)]
    return pl.pallas_call(
        kernel,
        out_shape=(
            jax.ShapeDtypeStruct((BOT // DP, COLS), F32),
            jax.ShapeDtypeStruct((BOT // DP, COLS), F32),
            jax.ShapeDtypeStruct((ROWS, BOT), F32),
            jax.ShapeDtypeStruct((ROWS, BOT), F32),
        ),
        in_specs=[pl.BlockSpec(memory_space=vmem)] * 6,
        out_specs=(pl.BlockSpec(memory_space=vmem),) * 4,
        scratch_shapes=[
            vmem((ROWS, COLS), F32), vmem((ROWS, COLS), F32), vmem((ROWS, COLS), F32),
            vmem((BOT, COLS), BF16), vmem((BOT, COLS), BF16), vmem((BOT, COLS), BF16),
            vmem((ROWS, BOT), BF16), vmem((ROWS, BOT), BF16), vmem((ROWS, BOT), BF16),
            vmem((BOT, ROWS), BF16), vmem((BOT, ROWS), BF16),
            vmem((ROWS, TILE), F32),
            vmem((ROWS, COLS), BF16), vmem((ROWS, COLS), BF16),
            vmem((1, 2 * ROWS), F32),
            vmem((ITERS, 1, COLS), F32), vmem((ITERS, DP, 1, COLS), F32),
            vmem((ITERS, 1, ROWS), F32), vmem((ITERS, 7, 1, ROWS), F32),
            vmem((ITERS, 1, ROWS), F32), vmem((ITERS, 8, 1, ROWS), F32),
            vmem((1, 2 * ROWS), F32), vmem((7, 1, 2 * ROWS), F32),
            vmem((1, 2 * ROWS), F32), vmem((8, 1, 2 * ROWS), F32),
            vmem((ROWS, 2 * BOT), F32), vmem((ROWS // 2, 2 * BOT), F32),
            vmem((ROWS // 2, 2 * BOT), F32), vmem((7, 32, 2 * BOT), F32),
            vmem((32, 2 * BOT), F32), vmem((4, 8, 2 * BOT), F32),
            vmem((8, 2 * BOT), F32), vmem((32, 2 * BOT), F32),
            vmem((7, 32, 2 * BOT), F32), vmem((8, 32, 2 * BOT), F32),
            vmem((DP, BOT // DP, 2 * COLS), F32), vmem((DP, BOT // DP, 2 * COLS), F32),
            *pairs(ITERS, DP), *pairs(ITERS + 1, 7), *pairs(ITERS + 1, 8), *pairs(1),
            *pairs(7), *pairs(4), *pairs(4), *pairs(7), *pairs(8), *pairs(DP),
        ],
        compiler_params=pltpu.CompilerParams(
            collective_id=0, has_side_effects=True, vmem_limit_bytes=56 * 1024 * 1024
        ),
        name="sinkhorn_step",
    )(*args)


def solution(mesh):
    placed = (
        P("dp", None), P("dp", None), P("dp", None),
        P(None, "proto"), P(None, "proto"), P(None, "proto"),
    )
    return jax.shard_map(
        on_device,
        mesh=mesh,
        in_specs=placed,
        out_specs=(P("dp", "proto"), P("dp", "proto"), P("dp", None), P("dp", None)),
        check_vma=False,
    )
```

time: 475 us -> 155 us (0.33)
  blocking collectives: 289 us -> 0 us
  Pallas kernels: 0 us -> 149 us
  waiting for transfers between devices: 128 us -> 0 us
  starting transfers between devices: 20.5 us -> 0 us
  matrix products: 17.7 us -> 0 us
  other arithmetic: 13 us -> 0 us
    all_to_all x5 -> x0, blocking collectives: 179 us -> none  [sent_to_all(): return lax.all_to_all(copies, axis, split_axis=0, concat_axis=0, tiled=True)]
    pallas_call x0 -> x1, Pallas kernels: none -> 149 us  [on_device(): pl.pallas_call(kernel, out_shape=(jax.ShapeDtypeStruct((BOT // DP, COLS),...]
    all_to_all x3 -> x0, waiting for transfers between devices: 128 us -> none  [the longest x2 127 us: sum_at_owner(): parts = lax.all_to_all(in_blocks(array, dim, peers), axis, 0, 0, tiled=True)]
    all_gather x2 -> x0, blocking collectives: 110 us -> none  [the longest x1 55.4 us: on_device(): lax.all_gather(small_out, 'proto', axis=0, tiled=True)]
    all_to_all x3 -> x0, starting transfers between devices: 20.5 us -> none  [the longest x2 12.9 us: sum_at_owner(): parts = lax.all_to_all(in_blocks(array, dim, peers), axis, 0, 0, tiled=True)]
    dot_general x13 -> x0, matrix products: 17.7 us -> none  [the longest x3 5.6 us: on_device(): local_rows = jnp.dot(energy, proto_scale, precision=lax.Precision.HIGHEST)]
    reduce_sum x15 -> x0, other arithmetic: 5.56 us -> none  [the longest x3 2.46 us: unit_columns(): jnp.sum(values * values, axis=0, keepdims=True) + 1e-12]
  transfers between devices with their start and end apart: 3 -> 0, of which waited for: 3 -> 0; matrix products, arithmetic and copies ran while one was open for 3% -> 0% of each run, Pallas kernels for 0% -> 0%
where the time goes in v1:
time: 155 us
  Pallas kernels  149 us (96%)
  local copies, waits for them, and re-layouts  4.86 us (3%)
    pallas_call x1, Pallas kernels, on_device(): pl.pallas_call(kernel, out_shape=(jax.ShapeDtypeStruct((BOT // DP, COLS),...  149 us
    unnamed x8, local copies, waits for them, and re-layouts  4.86 us

profile of v1, /device:TPU:1, one launch (start us, length us, event | category | flops | bytes accessed | tf_op | source)
XLA Modules:
  0.0 154.6 jit_solution(9050363604352953926)
XLA Ops:
  0.6 149.1 %sinkhorn_step.1 = (f32[16,1024]{1,0:T(8,128)}, f32[16,1024]{1,0:T(8,128)}, f32[512,256]{1,0:T(8,128)}, f32[512,256]{1,0:T(8,128)}) custom-call(bf16[512,256]{1,0:T(8,128)(2,1)} %tf.1, bf16[512,256]{1,0:T(8,128)(2,1)} %sf.1, bf16[512,256]{1,0:T(8,128)(2,1)} %lf.1, bf16[256,1024]{1,0:T(8,128)(2,1)} %tp.1, bf16[256,1024]{1,0:T(8,128)(2,1)} %sp.1, ...), custom_call_target="tpu_custom_call" | custom-call | tf_op jit(solution)/shard_map/sinkhorn_step/pallas_call | solution.py:357
  149.7 0.0 copy-start.1
  149.7 1.5 copy.14
  151.2 0.0 copy-done.1
  151.2 0.6 copy.15
  151.9 0.0 copy-start
  151.9 1.9 %copy.16 = f32[512,256]{1,0:T(8,128)} copy(f32[512,256]{1,0:T(8,128)} %get-tuple-element.10) | data formatting | bytes 1048576
  153.8 0.0 copy-done
  153.8 0.8 copy.17
Async XLA Ops:
  149.7 1.5 copy-start.1
  151.9 1.9 %copy-start = (f32[512,256]{1,0:T(8,128)S(1)}, f32[512,256]{1,0:T(8,128)}, u32[]{:S(2)}) copy-start(f32[512,256]{1,0:T(8,128)} %get-tuple-element.11) | copy-start | bytes 1572868
